TPU v7x, 32 devices: a whole 2x2x4 slice. The times are simulated.
32 devices in a mesh: narrow: 2 (over x), wide: 16 (over z, y, core).
Axes of the slice: x: 2, y: 2, z: 4, core: 2. Of those that a mesh axis runs over, the one named last changes fastest.
Arguments:
- patches: bfloat16 [64, 256, 1152], P(('narrow', 'wide')), may hold values from -6 to 6
- condition: float32 [64, 1152], P(('narrow', 'wide')), may hold values from -6 to 6
- image_counts: int32 [32], P(('narrow', 'wide')), may hold values from 1 to 2, as said below
- ada_weight: bfloat16 [1152, 6912], P(None, 'wide'), may hold values from -0.1875 to 0.1875
- ada_bias: bfloat16 [6912], P('wide'), may hold values from -3 to 3
- inproj_weight: bfloat16 [1152, 3456], P('wide'), may hold values from -0.1875 to 0.1875
- inproj_bias: bfloat16 [2304], P('wide'), may hold values from -2 to 2
- outproj_weight: bfloat16 [1152, 1152], P('wide'), may hold values from -0.75 to 0.75
- outproj_bias: bfloat16 [1152], P('wide'), may hold values from -2 to 2
- up_weight: bfloat16 [1152, 4608], P('wide'), may hold values from -0.1875 to 0.1875
- up_bias: bfloat16 [4608], P('wide'), may hold values from -3 to 3
- down_weight: bfloat16 [4608, 1152], P('wide'), may hold values from -0.09375 to 0.09375
- down_bias: bfloat16 [1152], P('wide'), may hold values from -2 to 2
- cotangent: bfloat16 [64, 256, 1152], P(('narrow', 'wide')), may hold values from -6 to 6
Outputs:
- output: bfloat16 [64, 256, 1152], P(('narrow', 'wide'))
- grad_patches: bfloat16 [64, 256, 1152], P(('narrow', 'wide'))
- grad_condition: float32 [64, 1152], P(('narrow', 'wide'))
- grad_ada_weight: float32 [1152, 6912], P(None, 'wide')
- grad_ada_bias: float32 [6912], P('wide')
- grad_inproj_weight: float32 [1152, 3456], P('wide')
- grad_inproj_bias: float32 [2304], P('wide')
- grad_outproj_weight: float32 [1152, 1152], P('wide')
- grad_outproj_bias: float32 [1152], P('wide')
- grad_up_weight: float32 [1152, 4608], P('wide')
- grad_up_bias: float32 [4608], P('wide')
- grad_down_weight: float32 [4608, 1152], P('wide')
- grad_down_bias: float32 [1152], P('wide')
Inputs may be any that keep to these rules, and one draw needn't show every extreme that they name: `image_counts`: each device's number of live image slots; a device's live slots are its first ones. In every draw some device has 2 and some device has 1.
All inputs are finite; a program needn't handle non-finite values.
Results may differ from a plain program's by a relative error of at most 0.02.
The roundings to bfloat16 on the way count: a program that leaves them out, or rounds other values in their place, can miss the bound.
Values may be sent and summed in bfloat16 or wider, within the bound.
A program may use at most 192 MiB of HBM per device.

v0:
```python
from functools import partial
import jax
import jax.numpy as jnp
from jax import lax
from jax.sharding import PartitionSpec as P

HEADS = 16
norm_eps = 1e-06


def normalize(values):
    center = jnp.mean(values, axis=-1, keepdims=True)
    shifted = values - center
    inv_std = lax.rsqrt(jnp.mean(shifted * shifted, axis=-1, keepdims=True) + norm_eps)
    return (shifted * inv_std, inv_std)


def normalize_reverse(normed, inv_std, grad_normed):
    mean_grad = jnp.mean(grad_normed, axis=-1, keepdims=True)
    mean_proj = jnp.mean(grad_normed * normed, axis=-1, keepdims=True)
    return inv_std * (grad_normed - mean_grad - normed * mean_proj)


def matmul_rows(left, right):
    return jnp.dot(left, right, preferred_element_type=jnp.float32)


def matmul_back(left, right):
    return lax.dot_general(
        left, right, (((1,), (1,)), ((), ())), preferred_element_type=jnp.float32
    )


def matmul_outer(left, right):
    return lax.dot_general(
        left, right, (((0,), (0,)), ((), ())), preferred_element_type=jnp.float32
    )


def block_term(factors, count, first, width):
    pieces = []
    for left, right, base in factors:
        lower = max(first, base)
        upper = min(first + width, base + right.shape[1])
        if lower < upper:
            rows_part = lax.slice_in_dim(left, 0, count, axis=1)
            pieces.append(matmul_outer(rows_part, right[:, lower - base : upper - base]))
    return jnp.concatenate(pieces, axis=1)


def per_device(
    patches,
    condition,
    image_counts,
    ada_weight,
    ada_bias,
    inproj_weight,
    inproj_bias,
    outproj_weight,
    outproj_bias,
    up_weight,
    up_bias,
    down_weight,
    down_bias,
    cotangent,
):
    slots, seq_len, model_width = patches.shape
    head_dim = model_width // HEADS
    scale_qk = head_dim ** (-0.5)
    row_total = slots * seq_len
    wide_count = lax.axis_size("wide")
    live = (jnp.arange(slots) < image_counts[0]).astype(jnp.float32)[:, None, None]
    cond_act = jax.nn.silu(condition).astype(jnp.bfloat16)
    cond_all = lax.all_gather(cond_act, "wide", axis=0, tiled=True)
    mod_part = (matmul_rows(cond_all, ada_weight) + ada_bias.astype(jnp.float32)).astype(
        jnp.bfloat16
    )
    modulation = lax.all_to_all(mod_part, "wide", split_axis=0, concat_axis=1, tiled=True).astype(
        jnp.float32
    )
    segment_list = [
        modulation[:, None, number * model_width : (number + 1) * model_width]
        for number in range(6)
    ]
    (
        selfattn_offset,
        selfattn_scale,
        selfattn_gate,
        perceptron_offset,
        perceptron_scale,
        perceptron_gate,
    ) = segment_list
    fetched = (
        lax.all_gather(inproj_weight, "wide", axis=0, tiled=True),
        lax.all_gather(inproj_bias, "wide", axis=0, tiled=True),
        lax.all_gather(outproj_weight, "wide", axis=0, tiled=True),
        lax.all_gather(outproj_bias, "wide", axis=0, tiled=True),
        lax.all_gather(up_weight, "wide", axis=0, tiled=True),
        lax.all_gather(up_bias, "wide", axis=0, tiled=True),
        lax.all_gather(down_weight, "wide", axis=0, tiled=True),
        lax.all_gather(down_bias, "wide", axis=0, tiled=True),
    )
    w_inproj, b_inproj, w_outproj, b_outproj, w_up, b_up, w_down, b_down = fetched
    input_rows = patches.astype(jnp.float32)
    normalized_first, inverse_deviation = normalize(input_rows)
    first_input = (
        (normalized_first * (1.0 + selfattn_scale) + selfattn_offset)
        .astype(jnp.bfloat16)
        .reshape(row_total, model_width)
    )
    proj_bias = b_inproj.astype(jnp.float32)
    full_bias = jnp.concatenate(
        [proj_bias[:model_width], jnp.zeros((model_width,), jnp.float32), proj_bias[model_width:]]
    )
    projected = (matmul_rows(first_input, w_inproj) + full_bias).astype(jnp.bfloat16)
    query_rows = projected[:, :model_width].reshape(slots, seq_len, HEADS, head_dim)
    key_rows = projected[:, model_width : 2 * model_width].reshape(slots, seq_len, HEADS, head_dim)
    value_rows = projected[:, 2 * model_width :].reshape(slots, seq_len, HEADS, head_dim)
    scores = (
        jnp.einsum("sqhe,skhe->shqk", query_rows, key_rows, preferred_element_type=jnp.float32)
        * scale_qk
    )
    log_total = jax.nn.logsumexp(scores, axis=-1, keepdims=True)
    probs = jnp.exp(scores - log_total).astype(jnp.bfloat16)
    attended = jnp.einsum("shqk,skhe->sqhe", probs, value_rows, preferred_element_type=jnp.float32)
    attended = attended.astype(jnp.bfloat16).reshape(row_total, model_width)
    residual_branch = (matmul_rows(attended, w_outproj) + b_outproj.astype(jnp.float32)).reshape(
        slots, seq_len, model_width
    )
    between_state = input_rows + selfattn_gate * residual_branch
    normed_b, inv_b = normalize(between_state)
    second_in = (
        (normed_b * (1.0 + perceptron_scale) + perceptron_offset)
        .astype(jnp.bfloat16)
        .reshape(row_total, model_width)
    )
    hidden = matmul_rows(second_in, w_up) + b_up.astype(jnp.float32)
    gelu_value, gelu_pull = jax.vjp(partial(jax.nn.gelu, approximate=True), hidden)
    activated = gelu_value.astype(jnp.bfloat16)
    mlp_out = (matmul_rows(activated, w_down) + b_down.astype(jnp.float32)).reshape(
        slots, seq_len, model_width
    )
    output = ((between_state + perceptron_gate * mlp_out) * live).astype(jnp.bfloat16)
    back_weights = (
        lax.all_gather(inproj_weight, "wide", axis=0, tiled=True),
        lax.all_gather(inproj_bias, "wide", axis=0, tiled=True),
        lax.all_gather(outproj_weight, "wide", axis=0, tiled=True),
        lax.all_gather(outproj_bias, "wide", axis=0, tiled=True),
        lax.all_gather(up_weight, "wide", axis=0, tiled=True),
        lax.all_gather(up_bias, "wide", axis=0, tiled=True),
        lax.all_gather(down_weight, "wide", axis=0, tiled=True),
        lax.all_gather(down_bias, "wide", axis=0, tiled=True),
    )
    wb_inproj, _, wb_outproj, _, wb_up, _, wb_down, _ = back_weights
    grad_out = cotangent.astype(jnp.float32) * live
    grad_gate_mlp = jnp.sum(grad_out * mlp_out, axis=1)
    grad_mlp = (grad_out * perceptron_gate).astype(jnp.bfloat16).reshape(row_total, model_width)
    grad_down_bias = jnp.sum(grad_mlp.astype(jnp.float32), axis=0)
    grad_act = matmul_back(grad_mlp, wb_down)
    grad_hidden = gelu_pull(grad_act)[0].astype(jnp.bfloat16)
    grad_up_bias = jnp.sum(grad_hidden.astype(jnp.float32), axis=0)
    grad_second = matmul_back(grad_hidden, wb_up).reshape(slots, seq_len, model_width)
    grad_scale_mlp = jnp.sum(grad_second * normed_b, axis=1)
    grad_shift_mlp = jnp.sum(grad_second, axis=1)
    between_gradient = grad_out + normalize_reverse(
        normed_b, inv_b, grad_second * (1.0 + perceptron_scale)
    )
    selfattn_gate_gradient = jnp.sum(between_gradient * residual_branch, axis=1)
    residual_branch_gradient = (
        (between_gradient * selfattn_gate).astype(jnp.bfloat16).reshape(row_total, model_width)
    )
    grad_outproj_bias = jnp.sum(residual_branch_gradient.astype(jnp.float32), axis=0)
    grad_attended = (
        matmul_back(residual_branch_gradient, wb_outproj)
        .astype(jnp.bfloat16)
        .reshape(slots, seq_len, HEADS, head_dim)
    )
    scores_again = (
        jnp.einsum("sqhe,skhe->shqk", query_rows, key_rows, preferred_element_type=jnp.float32)
        * scale_qk
    )
    probs_full = jnp.exp(scores_again - log_total)
    grad_values = jnp.einsum(
        "shqk,sqhe->skhe",
        probs_full.astype(jnp.bfloat16),
        grad_attended,
        preferred_element_type=jnp.float32,
    )
    grad_probs = jnp.einsum(
        "sqhe,skhe->shqk", grad_attended, value_rows, preferred_element_type=jnp.float32
    )
    row_dot = jnp.sum(grad_probs * probs_full, axis=-1, keepdims=True)
    grad_scores = (probs_full * (grad_probs - row_dot)).astype(jnp.bfloat16)
    grad_queries = (
        jnp.einsum("shqk,skhe->sqhe", grad_scores, key_rows, preferred_element_type=jnp.float32)
        * scale_qk
    )
    grad_keys = (
        jnp.einsum("shqk,sqhe->skhe", grad_scores, query_rows, preferred_element_type=jnp.float32)
        * scale_qk
    )
    grad_projected = jnp.concatenate(
        [
            grad_queries.reshape(row_total, model_width),
            grad_keys.reshape(row_total, model_width),
            grad_values.reshape(row_total, model_width),
        ],
        axis=1,
    ).astype(jnp.bfloat16)
    proj_sums = jnp.sum(grad_projected.astype(jnp.float32), axis=0)
    grad_inproj_bias = jnp.concatenate([proj_sums[:model_width], proj_sums[2 * model_width :]])
    first_gradient = matmul_back(grad_projected, wb_inproj).reshape(slots, seq_len, model_width)
    selfattn_scale_gradient = jnp.sum(first_gradient * normalized_first, axis=1)
    selfattn_offset_gradient = jnp.sum(first_gradient, axis=1)
    grad_patches = (
        between_gradient
        + normalize_reverse(
            normalized_first, inverse_deviation, first_gradient * (1.0 + selfattn_scale)
        )
    ).astype(jnp.bfloat16)
    grad_modulation = jnp.concatenate(
        [
            selfattn_offset_gradient,
            selfattn_scale_gradient,
            selfattn_gate_gradient,
            grad_shift_mlp,
            grad_scale_mlp,
            grad_gate_mlp,
        ],
        axis=1,
    ).astype(jnp.bfloat16)
    grad_mod_part = lax.all_to_all(grad_modulation, "wide", split_axis=1, concat_axis=0, tiled=True)
    grad_ada_weight = matmul_outer(cond_all, grad_mod_part)
    grad_ada_bias = jnp.sum(grad_mod_part.astype(jnp.float32), axis=0)
    grad_cond_part = matmul_back(grad_mod_part, ada_weight)
    grad_cond_act = lax.psum_scatter(
        grad_cond_part.astype(jnp.bfloat16), "wide", scatter_dimension=0, tiled=True
    ).astype(jnp.float32)
    _, silu_pull = jax.vjp(jax.nn.silu, condition)
    grad_condition = silu_pull(grad_cond_act)[0]
    bias_shares = (
        lax.psum_scatter(
            grad_inproj_bias.astype(jnp.bfloat16), "wide", scatter_dimension=0, tiled=True
        ).astype(jnp.float32),
        lax.psum_scatter(
            grad_outproj_bias.astype(jnp.bfloat16), "wide", scatter_dimension=0, tiled=True
        ).astype(jnp.float32),
        lax.psum_scatter(
            grad_up_bias.astype(jnp.bfloat16), "wide", scatter_dimension=0, tiled=True
        ).astype(jnp.float32),
        lax.psum_scatter(
            grad_down_bias.astype(jnp.bfloat16), "wide", scatter_dimension=0, tiled=True
        ).astype(jnp.float32),
    )
    ff_width = activated.shape[1]
    input_factors = (
        (first_input, grad_projected, 0),
        (attended, residual_branch_gradient, 3 * model_width),
        (second_in, grad_hidden, 4 * model_width),
    )
    down_factors = ((activated, grad_mlp, 0),)
    input_block = (4 * model_width + ff_width) // 4
    down_block = model_width // 2
    block_jobs = [
        (input_factors, model_width, number * input_block, input_block) for number in range(4)
    ]
    block_jobs = block_jobs + [
        (down_factors, ff_width, number * down_block, down_block) for number in range(2)
    ]

    def reduce_block(factors, rows, first, width):
        return lax.psum_scatter(
            block_term(factors, lax.axis_size("wide") * (rows // wide_count), first, width).astype(
                jnp.bfloat16
            ),
            "wide",
            scatter_dimension=0,
            tiled=True,
        ).astype(jnp.float32)

    shards = [reduce_block(*job) for job in block_jobs]
    input_grads = jnp.concatenate(shards[:4], axis=1)
    grad_down_weight = jnp.concatenate(shards[4:], axis=1)
    summed = (
        lax.psum(grad_ada_weight.astype(jnp.bfloat16), "narrow").astype(jnp.float32),
        lax.psum(grad_ada_bias.astype(jnp.bfloat16), "narrow").astype(jnp.float32),
        lax.psum(input_grads[:, : 3 * model_width].astype(jnp.bfloat16), "narrow").astype(
            jnp.float32
        ),
        lax.psum(bias_shares[0].astype(jnp.bfloat16), "narrow").astype(jnp.float32),
        lax.psum(
            input_grads[:, 3 * model_width : 4 * model_width].astype(jnp.bfloat16), "narrow"
        ).astype(jnp.float32),
        lax.psum(bias_shares[1].astype(jnp.bfloat16), "narrow").astype(jnp.float32),
        lax.psum(input_grads[:, 4 * model_width :].astype(jnp.bfloat16), "narrow").astype(
            jnp.float32
        ),
        lax.psum(bias_shares[2].astype(jnp.bfloat16), "narrow").astype(jnp.float32),
        lax.psum(grad_down_weight.astype(jnp.bfloat16), "narrow").astype(jnp.float32),
        lax.psum(bias_shares[3].astype(jnp.bfloat16), "narrow").astype(jnp.float32),
    )
    return (
        output,
        grad_patches,
        grad_condition,
        summed[0],
        summed[1],
        summed[2],
        summed[3],
        summed[4],
        summed[5],
        summed[6],
        summed[7],
        summed[8],
        summed[9],
    )


def solution(mesh):
    in_specs = (
        P(("narrow", "wide"), None, None),
        P(("narrow", "wide"), None),
        P(("narrow", "wide")),
        P(None, "wide"),
        P("wide"),
        P("wide", None),
        P("wide"),
        P("wide", None),
        P("wide"),
        P("wide", None),
        P("wide"),
        P("wide", None),
        P("wide"),
        P(("narrow", "wide"), None, None),
    )
    out_specs = (
        P(("narrow", "wide"), None, None),
        P(("narrow", "wide"), None, None),
        P(("narrow", "wide"), None),
        P(None, "wide"),
        P("wide"),
        P("wide", None),
        P("wide"),
        P("wide", None),
        P("wide"),
        P("wide", None),
        P("wide"),
        P("wide", None),
        P("wide"),
    )
    return jax.shard_map(
        per_device, mesh=mesh, in_specs=in_specs, out_specs=out_specs, check_vma=False
    )
```

profile of v0, /device:TPU:0, one launch (start us, length us, event | category | flops | bytes accessed | tf_op | source)
XLA Modules:
  0.0 1013.1 jit_solution(17286262413155684345)
XLA Ops:
  10.9 23.9 %all-gather = bf16[16,2,1152]{2,1,0:T(2,128)(2,1)S(1)} all-gather(bf16[1,2,1152]{2,1,0:T(2,128)(2,1)S(1)} %fusion.42), channel_id=1, replica_groups=mesh['narrow'=2,'wide'=16] {'wide'}, dimensions={0}, use_global_device_ids=true | all-gather | bytes 78336 | tf_op jit(solution)/shard_map/all_gather | solution.py:74
  44.1 64.5 %all-reduce.10 = (bf16[2304]{0:T(1024)(128)(2,1)S(1)}, bf16[1152]{0:T(1024)(128)(2,1)S(1)}, bf16[4608]{0:T(1024)(128)(2,1)S(1)}) all-reduce(bf16[2304]{0:T(1024)(128)(2,1)S(1)} %dynamic-update-slice, bf16[1152]{0:T(1024)(128)(2,1)S(1)} %dynamic-update-slice.1, ...), channel_id=1, replica_groups=mesh['narrow'=2,'wide'=16] {'wide'}, use_global_device_ids=true, to_apply=%add | all-reduce | flops 8064 | bytes 32256
  116.3 8.9 add_convert_fusion
  127.1 5.0 reshape.221
  134.6 5.7 reshape.222
  143.5 4.7 reshape.220
  168.5 50.5 %all-gather.10.cloned.1.call-done = bf16[1152,4608]{1,0:T(8,128)(2,1)} async-done(((bf16[72,4608]{1,0:T(8,128)(2,1)}), bf16[1152,4608]{1,0:T(8,128)(2,1)}) %all-gather.10.cloned.1.call-update) | async-done | bytes 10616848 | tf_op jit(solution)/shard_map/all_gather | solution.py:98
  219.0 13.7 %multiply_convert_fusion = (bf16[512,4608]{1,0:T(8,128)(2,1)}, f32[512,4608]{1,0:T(8,128)}) fusion(f32[4608]{0:T(1024)S(1)} %copy-done.51, bf16[512,1152]{1,0:T(8,128)(2,1)} %bitcast.131, bf16[1152,4608]{1,0:T(8,128)(2,1)} %all-gather.10.cloned.1.call-done), kind=kOutput, calls=%fused_computation.12 | convolution fusion | flops 5459410944 | bytes 25970688 | tf_op jit(solution)/shard_map/dot_general | solution.py:25
  232.7 75.1 %all-gather.12.cloned.1.call-done = bf16[4608,1152]{1,0:T(8,128)(2,1)} async-done(((bf16[288,1152]{1,0:T(8,128)(2,1)}), bf16[4608,1152]{1,0:T(8,128)(2,1)}) %all-gather.12.cloned.1.call-update) | async-done | bytes 10616848 | tf_op jit(solution)/shard_map/all_gather | solution.py:100
  307.8 15.9 %fusion.47 = (bf16[4608]{0:T(1024)(128)(2,1)S(1)}, bf16[512,4608]{1,0:T(8,128)(2,1)S(1)}) fusion(f32[512,4608]{1,0:T(8,128)} %get-tuple-element.67, f32[4608]{0:T(1024)S(1)} %copy-done.51, bf16[512,1152]{1,0:T(8,128)(2,1)} %bitcast.125, bf16[4608,1152]{1,0:T(8,128)(2,1)} %all-gather.12.cloned.1.call-done), kind=kOutput, calls=%fused_computation.124 | convolution fusion | flops 5487717888 | bytes 25979904 | tf_op jit(solution)/shard_map/dot_general | solution.py:29
  325.9 5.0 convolution_convert_fusion.1
  331.0 7.4 convolution_convert_fusion
  338.5 13.8 %fusion.29 = (f32[512]{0:T(512)S(1)}, f32[512,1152]{1,0:T(8,128)}) fusion(f32[2,1152]{1,0:T(2,128)S(1)} %get-tuple-element.52, bf16[512,4608]{1,0:T(8,128)(2,1)} %copy-done.60, bf16[1152,4608]{1,0:T(8,128)(2,1)} %all-gather.10.cloned.1.call-done), kind=kOutput, calls=%fused_computation.56 | convolution fusion | flops 5436997120 | bytes 17705984 | tf_op jit(solution)/shard_map/dot_general | solution.py:29
  363.3 5.7 reshape.223
  373.1 6.4 multiply_reduce_fusion
  379.6 4.8 multiply_convert_fusion.1
  390.6 5.9 convolution_convert_fusion.2
  396.8 5.4 fusion.32
  410.1 8.9 convolution_convert_fusion.4
  419.3 9.4 convolution_convert_fusion.3
  436.9 61.5 %all-reduce.9 = (bf16[1152]{0:T(1024)(128)(2,1)S(1)}, bf16[2304]{0:T(1024)(128)(2,1)S(1)}, bf16[1152]{0:T(1024)(128)(2,1)S(1)}, bf16[4608]{0:T(1024)(128)(2,1)S(1)}, bf16[1152]{0:T(1024)(128)(2,1)S(1)}) all-reduce(bf16[1152]{0:T(1024)(128)(2,1)S(1)} %dynamic-update-slice.3, ...), channel_id=1, replica_groups=mesh['narrow'=2,'wide'=16] {'wide'}, use_global_device_ids=true, to_apply=%add.3 | all-reduce | flops 10368 | bytes 41472
  498.4 10.4 %fusion.28 = (f32[512]{0:T(512)S(1)}, f32[512,1152]{1,0:T(8,128)S(1)}) fusion(f32[2,1152]{1,0:T(2,128)S(1)} %copy-done.42, bf16[512,3456]{0,1:T(8,128)(2,1)} %constant_dynamic-update-slice_fusion, bf16[1152,3456]{1,0:T(8,128)(2,1)} %all-gather.6.cloned.1.call-done), kind=kOutput, calls=%fused_computation.53 | convolution fusion | flops 4078042624 | bytes 13872128 | tf_op jit(solution)/shard_map/dot_general | solution.py:29
  510.3 10.1 convolution_add_fusion
  522.4 9.9 all_to_all.29
  536.7 33.8 %reduce-scatter.7.cloned.1.call-done = bf16[72,2304]{1,0:T(8,128)(2,1)} async-done(((bf16[1152,2304]{1,0:T(8,128)(2,1)}), bf16[72,2304]{1,0:T(8,128)(2,1)}) %reduce-scatter.7.cloned.1.call-update) | async-done | bytes 331792 | tf_op jit(solution)/shard_map/reduce_scatter | solution.py:272
  570.5 81.2 %reduce-scatter.9.cloned.1.call-done = bf16[72,2304]{1,0:T(8,128)(2,1)} async-done(((bf16[1152,2304]{1,0:T(8,128)(2,1)}), bf16[72,2304]{1,0:T(8,128)(2,1)}) %reduce-scatter.9.cloned.1.call-update) | async-done | bytes 331792 | tf_op jit(solution)/shard_map/reduce_scatter | solution.py:272
  653.6 83.5 %reduce-scatter.15.cloned.1.call-done = bf16[288,576]{1,0:T(8,128)(2,1)} async-done(((bf16[4608,576]{1,0:T(8,128)(2,1)}), bf16[288,576]{1,0:T(8,128)(2,1)}) %reduce-scatter.15.cloned.1.call-update) | async-done | bytes 331792 | tf_op jit(solution)/shard_map/reduce_scatter | solution.py:272
  737.1 85.3 %reduce-scatter.17.cloned.1.call-done = bf16[288,576]{1,0:T(8,128)(2,1)} async-done(((bf16[4608,576]{1,0:T(8,128)(2,1)}), bf16[288,576]{1,0:T(8,128)(2,1)}) %reduce-scatter.17.cloned.1.call-update) | async-done | bytes 331792 | tf_op jit(solution)/shard_map/reduce_scatter | solution.py:272
  828.2 4.3 fusion.20
  832.5 4.9 all-reduce.11
  840.2 71.8 %all-reduce.16.cloned.1.call-done = bf16[32,1152]{1,0:T(8,128)(2,1)} async-done(((bf16[32,1152]{1,0:T(8,128)(2,1)}), bf16[32,1152]{1,0:T(8,128)(2,1)}) %all-reduce.16.cloned.1.call-update) | async-done | bytes 73744
  913.3 85.7 %all-reduce.18.cloned.1.call-done = (bf16[1152,432]{0,1:T(8,128)(2,1)}, bf16[72,3456]{1,0:T(8,128)(2,1)}, bf16[72,1152]{1,0:T(8,128)(2,1)}, bf16[72,4608]{1,0:T(8,128)(2,1)}, bf16[288,1152]{1,0:T(8,128)(2,1)}) async-done(((bf16[1152,432]{0,1:T(8,128)(2,1)}, bf16[72,3456]{1,0:T(8,128)(2,1)}, bf16[72,1152]{1,0:T(8,128)(2,1)}, bf16[72,4608]{1,0:T(8,128)(2,1)}, bf16[288,1152]{1,0:T(8,128)(2,1)}), ...) | async-done | bytes 2986000 | tf_op jit(solution)/shard_map/psum | solution.py:285
  (261 shorter events, 109.7 us)
Async XLA Ops:
  7.2 28.3 %copy-start = (bf16[1152,432]{0,1:T(8,128)(2,1)S(1)}, bf16[1152,432]{0,1:T(8,128)(2,1)}, u32[]{:S(2)}) copy-start(bf16[1152,432]{0,1:T(8,128)(2,1)} %param.17) | copy-start | bytes 2985988
  7.2 32.9 %copy-start.55 = (u32[32]{0:T(128)S(1)}, u32[32]{0:T(128)}, u32[]{:S(2)}) copy-start(u32[32]{0:T(128)} %constant.56) | copy-start | bytes 388
  7.2 36.1 %copy-start.57 = (bf16[72]{0:T(256)(128)(2,1)S(1)}, bf16[72]{0:T(256)(128)(2,1)}, u32[]{:S(2)}) copy-start(bf16[72]{0:T(256)(128)(2,1)} %param.22) | copy-start | bytes 436
  7.2 36.4 %copy-start.56 = (bf16[288]{0:T(512)(128)(2,1)S(1)}, bf16[288]{0:T(512)(128)(2,1)}, u32[]{:S(2)}) copy-start(bf16[288]{0:T(512)(128)(2,1)} %param.24) | copy-start | bytes 1732
  7.2 36.6 %copy-start.58 = (bf16[144]{0:T(256)(128)(2,1)S(1)}, bf16[144]{0:T(256)(128)(2,1)}, u32[]{:S(2)}) copy-start(bf16[144]{0:T(256)(128)(2,1)} %param.20) | copy-start | bytes 868
  7.2 101.9 %copy-start.2 = (bf16[2,256,1152]{2,1,0:T(8,128)(2,1)S(1)}, bf16[2,256,1152]{2,1,0:T(8,128)(2,1)}, u32[]{:S(2)}) copy-start(bf16[2,256,1152]{2,1,0:T(8,128)(2,1)} %param.14) | copy-start | bytes 3538948
  7.2 109.0 %all-gather.6.cloned.1.call-start = ((), (), s32[]{:S(2)}) async-start(), calls=%async_computation.8 | async-start | bytes 8460288 | tf_op jit(solution)/shard_map/all_gather | solution.py:94
  8.0 152.9 %all-gather.8.cloned.1.call-start = ((), (), s32[]{:S(2)}) async-start(), calls=%async_computation.9 | async-start | bytes 2820096 | tf_op jit(solution)/shard_map/all_gather | solution.py:96
  8.7 210.3 %all-gather.10.cloned.1.call-start = ((), (), s32[]{:S(2)}) async-start(), calls=%async_computation.10 | async-start | bytes 11280384 | tf_op jit(solution)/shard_map/all_gather | solution.py:98
  9.5 298.3 %all-gather.12.cloned.1.call-start = ((), (), s32[]{:S(2)}) async-start(), calls=%async_computation.11 | async-start | bytes 11280384 | tf_op jit(solution)/shard_map/all_gather | solution.py:100
  10.0 102.9 %copy-start.15 = (bf16[2,256,1152]{2,1,0:T(8,128)(2,1)S(1)}, bf16[2,256,1152]{2,1,0:T(8,128)(2,1)}, u32[]{:S(2)}) copy-start(bf16[2,256,1152]{2,1,0:T(8,128)(2,1)} %param.27) | copy-start | bytes 3538948
  34.8 80.9 %copy-start.34 = (bf16[32,1152]{1,0:T(8,128)(2,1)}, bf16[32,1152]{1,0:T(8,128)(2,1)S(1)}, u32[]{:S(2)}) copy-start(bf16[32,1152]{1,0:T(8,128)(2,1)S(1)} %reshape.206) | copy-start | bytes 221188
  36.5 75.6 %all-to-all-start = ((bf16[16,2,432]{2,1,0:T(2,128)(2,1)}), bf16[16,2,432]{2,1,0:T(2,128)(2,1)S(1)}, u32[]{:S(2)}, u32[]{:S(2)}) async-start(bf16[16,2,432]{2,1,0:T(2,128)(2,1)} %all_to_all.22), calls=%async_computation | async-start | bytes 65536 | tf_op jit(solution)/shard_map/all_to_all | solution.py:78
  40.0 494.7 %reduce-scatter.11.cloned.1.call-start = ((), (), s32[]{:S(2)}) async-start(), calls=%async_computation.14 | async-start | bytes 5640192 | tf_op jit(solution)/shard_map/reduce_scatter | solution.py:272
  166.7 52.3 %copy-start.51 = (f32[4608]{0:T(1024)S(1)}, f32[4608]{0:T(1024)}, u32[]{:S(2)}) copy-start(f32[4608]{0:T(1024)} %convert_element_type.192) | copy-start | bytes 55300
  307.8 18.1 %copy-start.32 = (bf16[2,256,1152]{2,1,0:T(8,128)(2,1)S(1)}, bf16[2,256,1152]{2,1,0:T(8,128)(2,1)}, u32[]{:S(2)}) copy-start(bf16[2,256,1152]{2,1,0:T(8,128)(2,1)} %add_convert_fusion.1) | copy-start | bytes 3538948
  331.0 203.7 %reduce-scatter.13.cloned.1.call-start = ((), (), s32[]{:S(2)}) async-start(), calls=%async_computation.15 | async-start | bytes 5640192 | tf_op jit(solution)/shard_map/reduce_scatter | solution.py:272
  338.4 232.0 %reduce-scatter.7.cloned.1.call-start = ((), (), s32[]{:S(2)}) async-start(), calls=%async_computation.12 | async-start | bytes 5640192 | tf_op jit(solution)/shard_map/reduce_scatter | solution.py:272
  396.5 255.1 %reduce-scatter.9.cloned.1.call-start = ((), (), s32[]{:S(2)}) async-start(), calls=%async_computation.13 | async-start | bytes 5640192 | tf_op jit(solution)/shard_map/reduce_scatter | solution.py:272
  410.0 327.1 %reduce-scatter.15.cloned.1.call-start = ((), (), s32[]{:S(2)}) async-start(), calls=%async_computation.16 | async-start | bytes 6266880 | tf_op jit(solution)/shard_map/reduce_scatter | solution.py:272
  419.0 403.4 %reduce-scatter.17.cloned.1.call-start = ((), (), s32[]{:S(2)}) async-start(), calls=%async_computation.17 | async-start | bytes 6266880 | tf_op jit(solution)/shard_map/reduce_scatter | solution.py:272
  428.7 483.3 %all-reduce.16.cloned.1.call-start = ((), (), s32[]{:S(2)}) async-start(), calls=%async_computation.18 | async-start | bytes 147456
  434.3 64.1 %copy-start.42 = (f32[2,1152]{1,0:T(2,128)S(1)}, f32[2,1152]{1,0:T(2,128)}, u32[]{:S(2)}) copy-start(f32[2,1152]{1,0:T(2,128)} %copy-done.41) | copy-start | bytes 27652
  498.4 10.4 %copy-start.4 = (bf16[2,256,1152]{2,1,0:T(8,128)(2,1)S(1)}, bf16[2,256,1152]{2,1,0:T(8,128)(2,1)}, u32[]{:S(2)}) copy-start(bf16[2,256,1152]{2,1,0:T(8,128)(2,1)} %param.14) | copy-start | bytes 3538948
  498.4 10.4 %copy-start.46 = (f32[2,256]{1,0:T(2,128)S(1)}, f32[2,256]{1,0:T(2,128)}, u32[]{:S(2)}) copy-start(f32[2,256]{1,0:T(2,128)} %copy-done.45) | copy-start | bytes 6148
  498.4 10.4 %copy-start.50 = (f32[2,256]{1,0:T(2,128)S(1)}, f32[2,256]{1,0:T(2,128)}, u32[]{:S(2)}) copy-start(f32[2,256]{1,0:T(2,128)} %add_rsqrt_fusion.1) | copy-start | bytes 6148
  510.3 10.1 copy-start.17
  520.4 11.9 %copy-start.35 = (bf16[32,1152]{1,0:T(8,128)(2,1)S(1)}, bf16[32,1152]{1,0:T(8,128)(2,1)}, u32[]{:S(2)}) copy-start(bf16[32,1152]{1,0:T(8,128)(2,1)} %copy-done.34) | copy-start | bytes 221188
  534.6 464.4 %all-reduce.18.cloned.1.call-start = ((), (), s32[]{:S(2)}) async-start(), calls=%async_computation.19 | async-start | bytes 5971968 | tf_op jit(solution)/shard_map/psum | solution.py:285
  651.7 172.9 %copy-start.33 = (bf16[72,2304]{1,0:T(8,128)(2,1)S(1)}, bf16[72,2304]{1,0:T(8,128)(2,1)}, u32[]{:S(2)}) copy-start(bf16[72,2304]{1,0:T(8,128)(2,1)} %reduce-scatter.9.cloned.1.call-done) | copy-start | bytes 995332
  653.6 174.6 %copy-start.5 = (bf16[2,256,1152]{2,1,0:T(8,128)(2,1)S(1)}, bf16[2,256,1152]{2,1,0:T(8,128)(2,1)}, u32[]{:S(2)}) copy-start(bf16[2,256,1152]{2,1,0:T(8,128)(2,1)} %param.14) | copy-start | bytes 3538948
  828.2 83.8 %copy-start.47 = (f32[2,1152]{1,0:T(2,128)S(1)}, f32[2,1152]{1,0:T(2,128)}, u32[]{:S(2)}) copy-start(f32[2,1152]{1,0:T(2,128)} %param.15) | copy-start | bytes 27652
  (42 other events, 134.5 us)
Sparse Core Ops, SparseCore 0:
  10.2 75.2 all-gather.5
  87.7 41.8 all-gather.7
  131.9 87.1 all-gather.9
  221.2 86.5 all-gather.11
  331.1 76.3 reduce-scatter.10
  411.4 77.7 reduce-scatter.12
  493.3 77.1 reduce-scatter.6
  574.5 77.1 reduce-scatter.8
  655.6 81.4 reduce-scatter.14
  740.9 81.4 reduce-scatter.16
  825.9 86.0 all-reduce.15
  915.6 83.3 all-reduce.17
where the time goes:
time: 1020 us; the launch traced here: 1010 us
  waiting for transfers between devices  570 us (56%)
  blocking collectives  165 us (16%)
  matrix products  141 us (14%)
  local copies, waits for them, and re-layouts  60.7 us (6%)
  other arithmetic  51.8 us (5%)
  between operations  20.7 us (2%)
    reduce_scatter x6, waiting for transfers between devices, reduce_block(): lax.psum_scatter(block_term(factors, lax.axis_size('wide') * (rows // wid...  284 us
    unnamed x2, blocking collectives  126 us
    psum x1, waiting for transfers between devices, per_device(): lax.psum(grad_ada_weight.astype(jnp.bfloat16), 'narrow').astype(jnp.float32)  85.7 us
    all_gather x1, waiting for transfers between devices, per_device(): lax.all_gather(down_weight, 'wide', axis=0, tiled=True)  75.1 us
    unnamed x13, waiting for transfers between devices  74.6 us
    all_gather x1, waiting for transfers between devices, per_device(): lax.all_gather(up_weight, 'wide', axis=0, tiled=True)  50.5 us
    dot_general x5, matrix products, matmul_back(): lax.dot_general(left, right, (((1,), (1,)), ((), ())), preferred_element_...  43.9 us
    dot_general x8, matrix products, matmul_outer(): lax.dot_general(left, right, (((0,), (0,)), ((), ())), preferred_element_...  41.4 us
  transfers between devices with their start and end apart: 13, of which 8 were waited for; matrix products, arithmetic and copies ran while one was open for 21% of the time, Pallas kernels for 0%

commit v1 on v0

--- a/solution.py
+++ b/solution.py
@@ -6,6 +6,19 @@
 
 HEADS = 16
 norm_eps = 1e-06
+
+
+def collect(x, axis, dim):
+    ways = lax.axis_size(axis)
+    up = [(d, (d + 1) % ways) for d in range(ways)]
+    down = [(d, (d - 1) % ways) for d in range(ways)]
+    earlier, later = ([x], [x])
+    for _ in range(ways // 2):
+        earlier.append(lax.ppermute(earlier[-1], axis, up))
+    for _ in range((ways - 1) // 2):
+        later.append(lax.ppermute(later[-1], axis, down))
+    line = jnp.concatenate([*earlier[::-1], *later[1:]], axis=dim)
+    return jnp.roll(line, (lax.axis_index(axis) - ways // 2) * x.shape[dim], axis=dim)
 
 
 def normalize(values):
@@ -95,7 +108,7 @@
         lax.all_gather(inproj_bias, "wide", axis=0, tiled=True),
         lax.all_gather(outproj_weight, "wide", axis=0, tiled=True),
         lax.all_gather(outproj_bias, "wide", axis=0, tiled=True),
-        lax.all_gather(up_weight, "wide", axis=0, tiled=True),
+        collect(up_weight, "wide", 0),
         lax.all_gather(up_bias, "wide", axis=0, tiled=True),
         lax.all_gather(down_weight, "wide", axis=0, tiled=True),
         lax.all_gather(down_bias, "wide", axis=0, tiled=True),

time: 1020 us -> 1080 us (1.059)
  local copies, waits for them, and re-layouts: 60.7 us -> 112 us
  waiting for transfers between devices: 570 us -> 523 us
  starting transfers between devices: 4.45 us -> 39.7 us
  blocking collectives: 165 us -> 190 us
    ppermute x0 -> x15, waiting for transfers between devices: none -> 90.8 us  [the longest x8 63.4 us: collect(): earlier.append(lax.ppermute(earlier[-1], axis, up))]
    all_gather x1, waiting for transfers between devices: 75.1 us -> 0.02 us  [per_device(): lax.all_gather(down_weight, 'wide', axis=0, tiled=True)]
    all_gather x1, waiting for transfers between devices: 50.5 us -> 0.02 us  [per_device(): lax.all_gather(up_weight, 'wide', axis=0, tiled=True)]
    unnamed x147 -> x198, local copies, waits for them, and re-layouts: 17.1 us -> 66.4 us
    ppermute x0 -> x15, starting transfers between devices: none -> 35.5 us  [the longest x7 27.3 us: collect(): later.append(lax.ppermute(later[-1], axis, down))]
    unnamed x2, blocking collectives: 126 us -> 144 us
  transfers between devices with their start and end apart: 13 -> 28, of which waited for: 8 -> 13; matrix products, arithmetic and copies ran while one was open for 21% -> 26% of each run, Pallas kernels for 0% -> 0%
where the time goes in v1:
time: 1080 us
  waiting for transfers between devices  523 us (48%)
  blocking collectives  190 us (18%)
  matrix products  139 us (13%)
  local copies, waits for them, and re-layouts  112 us (10%)
  other arithmetic  51.6 us (5%)
  starting transfers between devices  39.7 us (4%)
  between operations  20.7 us (2%)
    reduce_scatter x6, waiting for transfers between devices, reduce_block(): lax.psum_scatter(block_term(factors, lax.axis_size('wide') * (rows // wid...  273 us
    unnamed x2, blocking collectives  144 us
    psum x1, waiting for transfers between devices, per_device(): lax.psum(grad_ada_weight.astype(jnp.bfloat16), 'narrow').astype(jnp.float32)  85.7 us
    unnamed x13, waiting for transfers between devices  73.7 us
    unnamed x198, local copies, waits for them, and re-layouts  66.4 us
    ppermute x8, waiting for transfers between devices, collect(): earlier.append(lax.ppermute(earlier[-1], axis, up))  63.4 us
    dot_general x5, matrix products, matmul_back(): lax.dot_general(left, right, (((1,), (1,)), ((), ())), preferred_element_...  42.9 us
    dot_general x5, matrix products, matmul_rows(): return jnp.dot(left, right, preferred_element_type=jnp.float32)  39.9 us
  transfers between devices with their start and end apart: 28, of which 13 were waited for; matrix products, arithmetic and copies ran while one was open for 26% of the time, Pallas kernels for 0%

profile of v1, /device:TPU:0, one launch (start us, length us, event | category | flops | bytes accessed | tf_op | source)
XLA Modules:
  0.0 1076.8 jit_solution(8513776396981056455)
XLA Ops:
  10.0 13.6 %collective-permute-done = bf16[72,4608]{1,0:T(8,128)(2,1)S(1)} collective-permute-done((bf16[72,4608]{1,0:T(8,128)(2,1)}, bf16[72,4608]{1,0:T(8,128)(2,1)S(1)}, u32[]{:S(2)}, u32[]{:S(2)}) %collective-permute-start) | collective-permute-done | bytes 663584 | tf_op jit(solution)/shard_map/ppermute | solution.py:17
  28.9 21.1 %collective-permute-done.1 = bf16[72,4608]{1,0:T(8,128)(2,1)S(1)} collective-permute-done((bf16[72,4608]{1,0:T(8,128)(2,1)S(1)}, bf16[72,4608]{1,0:T(8,128)(2,1)S(1)}, u32[]{:S(2)}, u32[]{:S(2)}) %collective-permute-start.1) | collective-permute-done | bytes 663584 | tf_op jit(solution)/shard_map/ppermute | solution.py:17
  55.3 19.6 %collective-permute-done.2 = bf16[72,4608]{1,0:T(8,128)(2,1)S(1)} collective-permute-done((bf16[72,4608]{1,0:T(8,128)(2,1)S(1)}, bf16[72,4608]{1,0:T(8,128)(2,1)S(1)}, u32[]{:S(2)}, u32[]{:S(2)}) %collective-permute-start.2) | collective-permute-done | bytes 663584 | tf_op jit(solution)/shard_map/ppermute | solution.py:17
  80.1 9.1 collective-permute-done.3
  89.2 31.1 %all-gather = bf16[16,2,1152]{2,1,0:T(2,128)(2,1)S(1)} all-gather(bf16[1,2,1152]{2,1,0:T(2,128)(2,1)S(1)} %fusion.44), channel_id=1, replica_groups=mesh['narrow'=2,'wide'=16] {'wide'}, dimensions={0}, use_global_device_ids=true | all-gather | bytes 78336 | tf_op jit(solution)/shard_map/all_gather | solution.py:87
  129.5 63.6 %all-reduce.10 = (bf16[2304]{0:T(1024)(128)(2,1)S(1)}, bf16[1152]{0:T(1024)(128)(2,1)S(1)}, bf16[4608]{0:T(1024)(128)(2,1)S(1)}) all-reduce(bf16[2304]{0:T(1024)(128)(2,1)S(1)} %dynamic-update-slice, bf16[1152]{0:T(1024)(128)(2,1)S(1)} %dynamic-update-slice.1, ...), channel_id=1, replica_groups=mesh['narrow'=2,'wide'=16] {'wide'}, use_global_device_ids=true, to_apply=%add | all-reduce | flops 8064 | bytes 32256
  209.8 19.9 %collective-permute-done.12 = bf16[72,4608]{1,0:T(8,128)(2,1)} collective-permute-done((bf16[72,4608]{1,0:T(8,128)(2,1)}, bf16[72,4608]{1,0:T(8,128)(2,1)}, u32[]{:S(2)}, u32[]{:S(2)}) %collective-permute-start.12) | collective-permute-done | bytes 663584 | tf_op jit(solution)/shard_map/ppermute | solution.py:19
  234.3 5.1 collective-permute-start.7
  297.7 8.8 add_convert_fusion
  308.5 5.0 reshape.221
  316.1 5.8 reshape.222
  349.1 16.6 %multiply_convert_fusion = (bf16[512,4608]{1,0:T(8,128)(2,1)S(1)}, f32[512,4608]{1,0:T(8,128)}) fusion(f32[4608]{0:T(1024)S(1)} %copy-done.60, bf16[512,1152]{1,0:T(8,128)(2,1)S(1)} %bitcast.130, bf16[2304,4608]{1,0:T(8,128)(2,1)} %constant_dynamic-update-slice_fusion, s32[]{:T(128)S(6)} %select_n.26), kind=kOutput, calls=%fused_computation.14 | convolution fusion | flops 5459410944 | bytes 25970692 | tf_op jit(solution)/shard_map/dot_general | solution.py:38
  367.8 5.7 convolution_convert_fusion.4
  373.6 8.9 convolution_convert_fusion.3
  382.6 16.0 %fusion.50 = (bf16[4608]{0:T(1024)(128)(2,1)S(1)}, bf16[512,4608]{1,0:T(8,128)(2,1)S(1)}) fusion(f32[512,4608]{1,0:T(8,128)} %get-tuple-element.67, f32[4608]{0:T(1024)S(1)} %copy-done.60, bf16[512,1152]{1,0:T(8,128)(2,1)} %bitcast.125, bf16[4608,1152]{1,0:T(8,128)(2,1)} %all-gather.10.cloned.1.call-done), kind=kOutput, calls=%fused_computation.159 | convolution fusion | flops 5487717888 | bytes 25979904 | tf_op jit(solution)/shard_map/dot_general | solution.py:42
  400.7 5.1 convolution_convert_fusion.1
  405.9 7.6 convolution_convert_fusion
  413.5 12.8 %fusion.31 = (f32[512]{0:T(512)S(1)}, f32[512,1152]{1,0:T(8,128)}) fusion(f32[2,1152]{1,0:T(2,128)S(1)} %get-tuple-element.52, bf16[512,4608]{1,0:T(8,128)(2,1)} %copy-done.69, bf16[1152,4608]{1,0:T(8,128)(2,1)} %all-gather.12.cloned.1.call-done), kind=kOutput, calls=%fused_computation.58 | convolution fusion | flops 5436997120 | bytes 17705984 | tf_op jit(solution)/shard_map/dot_general | solution.py:42
  437.4 5.7 reshape.223
  447.2 6.3 multiply_reduce_fusion
  464.5 6.0 convolution_convert_fusion.2
  470.8 5.4 fusion.34
  492.6 80.7 %all-reduce.9 = (bf16[1152]{0:T(1024)(128)(2,1)S(1)}, bf16[2304]{0:T(1024)(128)(2,1)S(1)}, bf16[1152]{0:T(1024)(128)(2,1)S(1)}, bf16[4608]{0:T(1024)(128)(2,1)S(1)}, bf16[1152]{0:T(1024)(128)(2,1)S(1)}) all-reduce(bf16[1152]{0:T(1024)(128)(2,1)S(1)} %dynamic-update-slice.3, ...), channel_id=1, replica_groups=mesh['narrow'=2,'wide'=16] {'wide'}, use_global_device_ids=true, to_apply=%add.3 | all-reduce | flops 10368 | bytes 41472
  573.3 10.4 fusion.30
  585.2 10.0 convolution_add_fusion
  597.2 9.5 all_to_all.29
  611.3 31.7 %reduce-scatter.11.cloned.1.call-done = bf16[72,2304]{1,0:T(8,128)(2,1)} async-done(((bf16[1152,2304]{1,0:T(8,128)(2,1)}), bf16[72,2304]{1,0:T(8,128)(2,1)}) %reduce-scatter.11.cloned.1.call-update) | async-done | bytes 331792 | tf_op jit(solution)/shard_map/reduce_scatter | solution.py:285
  643.0 81.2 %reduce-scatter.13.cloned.1.call-done = bf16[72,2304]{1,0:T(8,128)(2,1)} async-done(((bf16[1152,2304]{1,0:T(8,128)(2,1)}), bf16[72,2304]{1,0:T(8,128)(2,1)}) %reduce-scatter.13.cloned.1.call-update) | async-done | bytes 331792 | tf_op jit(solution)/shard_map/reduce_scatter | solution.py:285
  726.2 79.2 %reduce-scatter.7.cloned.1.call-done = bf16[72,2304]{1,0:T(8,128)(2,1)} async-done(((bf16[1152,2304]{1,0:T(8,128)(2,1)}), bf16[72,2304]{1,0:T(8,128)(2,1)}) %reduce-scatter.7.cloned.1.call-update) | async-done | bytes 331792 | tf_op jit(solution)/shard_map/reduce_scatter | solution.py:285
  805.4 81.0 %reduce-scatter.9.cloned.1.call-done = bf16[72,2304]{1,0:T(8,128)(2,1)} async-done(((bf16[1152,2304]{1,0:T(8,128)(2,1)}), bf16[72,2304]{1,0:T(8,128)(2,1)}) %reduce-scatter.9.cloned.1.call-update) | async-done | bytes 331792 | tf_op jit(solution)/shard_map/reduce_scatter | solution.py:285
  904.9 71.0 %all-reduce.16.cloned.1.call-done = bf16[32,1152]{1,0:T(8,128)(2,1)} async-done(((bf16[32,1152]{1,0:T(8,128)(2,1)}), bf16[32,1152]{1,0:T(8,128)(2,1)}) %all-reduce.16.cloned.1.call-update) | async-done | bytes 73744
  977.2 85.7 %all-reduce.18.cloned.1.call-done = (bf16[1152,432]{0,1:T(8,128)(2,1)}, bf16[72,3456]{1,0:T(8,128)(2,1)}, bf16[72,1152]{1,0:T(8,128)(2,1)}, bf16[72,4608]{1,0:T(8,128)(2,1)}, bf16[288,1152]{1,0:T(8,128)(2,1)}) async-done(((bf16[1152,432]{0,1:T(8,128)(2,1)}, bf16[72,3456]{1,0:T(8,128)(2,1)}, bf16[72,1152]{1,0:T(8,128)(2,1)}, bf16[72,4608]{1,0:T(8,128)(2,1)}, bf16[288,1152]{1,0:T(8,128)(2,1)}), ...) | async-done | bytes 2986000 | tf_op jit(solution)/shard_map/psum | solution.py:298
  (343 shorter events, 217.2 us)
Async XLA Ops:
  7.2 122.0 %copy-start.67 = (bf16[144]{0:T(256)(128)(2,1)S(1)}, bf16[144]{0:T(256)(128)(2,1)}, u32[]{:S(2)}) copy-start(bf16[144]{0:T(256)(128)(2,1)} %param.20) | copy-start | bytes 868
  7.2 185.9 %copy-start.2 = (bf16[2,256,1152]{2,1,0:T(8,128)(2,1)S(1)}, bf16[2,256,1152]{2,1,0:T(8,128)(2,1)}, u32[]{:S(2)}) copy-start(bf16[2,256,1152]{2,1,0:T(8,128)(2,1)} %param.14) | copy-start | bytes 3538948
  7.2 290.5 %all-gather.6.cloned.1.call-start = ((), (), s32[]{:S(2)}) async-start(), calls=%async_computation.8 | async-start | bytes 8460288 | tf_op jit(solution)/shard_map/all_gather | solution.py:107
  8.0 334.6 %all-gather.8.cloned.1.call-start = ((), (), s32[]{:S(2)}) async-start(), calls=%async_computation.9 | async-start | bytes 2820096 | tf_op jit(solution)/shard_map/all_gather | solution.py:109
  8.7 373.9 %all-gather.10.cloned.1.call-start = ((), (), s32[]{:S(2)}) async-start(), calls=%async_computation.10 | async-start | bytes 11280384 | tf_op jit(solution)/shard_map/all_gather | solution.py:113
  9.5 230.0 %copy-start.15 = (bf16[2,256,1152]{2,1,0:T(8,128)(2,1)S(1)}, bf16[2,256,1152]{2,1,0:T(8,128)(2,1)}, u32[]{:S(2)}) copy-start(bf16[2,256,1152]{2,1,0:T(8,128)(2,1)} %param.27) | copy-start | bytes 3538948
  9.5 14.1 %collective-permute-start = (bf16[72,4608]{1,0:T(8,128)(2,1)}, bf16[72,4608]{1,0:T(8,128)(2,1)S(1)}, u32[]{:S(2)}, u32[]{:S(2)}) collective-permute-start(bf16[72,4608]{1,0:T(8,128)(2,1)} %param.23), channel_id=1, source_target_pairs={{0,1},{1,2},{2,3},{3,4},{4,5},{5,6},{6,7},{7,8},{8,9},{9,10},{10,1... | collective-permute-start | bytes 1990664 | tf_op jit(solution)/shard_map/ppermute | solution.py:17
  24.4 25.5 %collective-permute-start.1 = (bf16[72,4608]{1,0:T(8,128)(2,1)S(1)}, bf16[72,4608]{1,0:T(8,128)(2,1)S(1)}, u32[]{:S(2)}, u32[]{:S(2)}) collective-permute-start(bf16[72,4608]{1,0:T(8,128)(2,1)S(1)} %collective-permute-done), channel_id=1, source_target_pairs={{0,1},{1,2},{2,3},{3,4},{4,5},{5,6},{6,7},{7,8},{8,9},{9,10},{10,1... | collective-permute-start | bytes 1990664 | tf_op jit(solution)/shard_map/ppermute | solution.py:17
  24.4 25.6 %collective-permute-start.8 = (bf16[72,4608]{1,0:T(8,128)(2,1)}, bf16[72,4608]{1,0:T(8,128)(2,1)S(1)}, u32[]{:S(2)}, u32[]{:S(2)}) collective-permute-start(bf16[72,4608]{1,0:T(8,128)(2,1)} %param.23), channel_id=1, source_target_pairs={{0,15},{1,0},{2,1},{3,2},{4,3},{5,4},{6,5},{7,6},{8,7},{9,8},{10,9... | collective-permute-start | bytes 1990664 | tf_op jit(solution)/shard_map/ppermute | solution.py:19
  50.0 24.9 %collective-permute-start.2 = (bf16[72,4608]{1,0:T(8,128)(2,1)S(1)}, bf16[72,4608]{1,0:T(8,128)(2,1)S(1)}, u32[]{:S(2)}, u32[]{:S(2)}) collective-permute-start(bf16[72,4608]{1,0:T(8,128)(2,1)S(1)} %collective-permute-done.1), channel_id=1, source_target_pairs={{0,1},{1,2},{2,3},{3,4},{4,5},{5,6},{6,7},{7,8},{8,9},{9,10},{10,1... | collective-permute-start | bytes 1990664 | tf_op jit(solution)/shard_map/ppermute | solution.py:17
  50.8 24.7 %collective-permute-start.9 = (bf16[72,4608]{1,0:T(8,128)(2,1)S(1)}, bf16[72,4608]{1,0:T(8,128)(2,1)}, u32[]{:S(2)}, u32[]{:S(2)}) collective-permute-start(bf16[72,4608]{1,0:T(8,128)(2,1)S(1)} %collective-permute-done.8), channel_id=1, source_target_pairs={{0,15},{1,0},{2,1},{3,2},{4,3},{5,4},{6,5},{7,6},{8,7},{9,8},{10,9... | collective-permute-start | bytes 1990664 | tf_op jit(solution)/shard_map/ppermute | solution.py:19
  74.9 14.3 %collective-permute-start.3 = (bf16[72,4608]{1,0:T(8,128)(2,1)S(1)}, bf16[72,4608]{1,0:T(8,128)(2,1)}, u32[]{:S(2)}, u32[]{:S(2)}) collective-permute-start(bf16[72,4608]{1,0:T(8,128)(2,1)S(1)} %collective-permute-done.2), channel_id=1, source_target_pairs={{0,1},{1,2},{2,3},{3,4},{4,5},{5,6},{6,7},{7,8},{8,9},{9,10},{10,1... | collective-permute-start | bytes 1990664 | tf_op jit(solution)/shard_map/ppermute | solution.py:17
  75.7 117.6 %collective-permute-start.10 = (bf16[72,4608]{1,0:T(8,128)(2,1)}, bf16[72,4608]{1,0:T(8,128)(2,1)}, u32[]{:S(2)}, u32[]{:S(2)}) collective-permute-start(bf16[72,4608]{1,0:T(8,128)(2,1)} %collective-permute-done.9), channel_id=1, source_target_pairs={{0,15},{1,0},{2,1},{3,2},{4,3},{5,4},{6,5},{7,6},{8,7},{9,8},{10,9... | collective-permute-start | bytes 1990664 | tf_op jit(solution)/shard_map/ppermute | solution.py:19
  89.2 104.2 %collective-permute-start.4 = (bf16[72,4608]{1,0:T(8,128)(2,1)}, bf16[72,4608]{1,0:T(8,128)(2,1)}, u32[]{:S(2)}, u32[]{:S(2)}) collective-permute-start(bf16[72,4608]{1,0:T(8,128)(2,1)} %collective-permute-done.3), channel_id=1, source_target_pairs={{0,1},{1,2},{2,3},{3,4},{4,5},{5,6},{6,7},{7,8},{8,9},{9,10},{10,1... | collective-permute-start | bytes 1990664 | tf_op jit(solution)/shard_map/ppermute | solution.py:17
  122.1 86.9 %all-to-all-start = ((bf16[16,2,432]{2,1,0:T(2,128)(2,1)}), bf16[16,2,432]{2,1,0:T(2,128)(2,1)S(1)}, u32[]{:S(2)}, u32[]{:S(2)}) async-start(bf16[16,2,432]{2,1,0:T(2,128)(2,1)} %all_to_all.22), calls=%async_computation | async-start | bytes 65536 | tf_op jit(solution)/shard_map/all_to_all | solution.py:91
  125.6 288.0 %all-gather.12.cloned.1.call-start = ((), (), s32[]{:S(2)}) async-start(), calls=%async_computation.11 | async-start | bytes 11280384 | tf_op jit(solution)/shard_map/all_gather | solution.py:162
  126.1 483.0 %reduce-scatter.15.cloned.1.call-start = ((), (), s32[]{:S(2)}) async-start(), calls=%async_computation.16 | async-start | bytes 6266880 | tf_op jit(solution)/shard_map/reduce_scatter | solution.py:285
  193.3 9.0 collective-permute-start.11
  193.4 13.5 %collective-permute-start.5 = (bf16[72,4608]{1,0:T(8,128)(2,1)}, bf16[72,4608]{1,0:T(8,128)(2,1)}, u32[]{:S(2)}, u32[]{:S(2)}) collective-permute-start(bf16[72,4608]{1,0:T(8,128)(2,1)} %collective-permute-done.4), channel_id=1, source_target_pairs={{0,1},{1,2},{2,3},{3,4},{4,5},{5,6},{6,7},{7,8},{8,9},{9,10},{10,1... | collective-permute-start | bytes 1990664 | tf_op jit(solution)/shard_map/ppermute | solution.py:17
  202.4 27.4 %collective-permute-start.12 = (bf16[72,4608]{1,0:T(8,128)(2,1)}, bf16[72,4608]{1,0:T(8,128)(2,1)}, u32[]{:S(2)}, u32[]{:S(2)}) collective-permute-start(bf16[72,4608]{1,0:T(8,128)(2,1)} %collective-permute-done.11), channel_id=1, source_target_pairs={{0,15},{1,0},{2,1},{3,2},{4,3},{5,4},{6,5},{7,6},{8,7},{9,8},{10,9... | collective-permute-start | bytes 1990664 | tf_op jit(solution)/shard_map/ppermute | solution.py:19
  207.0 27.4 %collective-permute-start.6 = (bf16[72,4608]{1,0:T(8,128)(2,1)}, bf16[72,4608]{1,0:T(8,128)(2,1)}, u32[]{:S(2)}, u32[]{:S(2)}) collective-permute-start(bf16[72,4608]{1,0:T(8,128)(2,1)} %collective-permute-done.5), channel_id=1, source_target_pairs={{0,1},{1,2},{2,3},{3,4},{4,5},{5,6},{6,7},{7,8},{8,9},{9,10},{10,1... | collective-permute-start | bytes 1990664 | tf_op jit(solution)/shard_map/ppermute | solution.py:17
  229.7 16.7 %collective-permute-start.13 = (bf16[72,4608]{1,0:T(8,128)(2,1)}, bf16[72,4608]{1,0:T(8,128)(2,1)S(1)}, u32[]{:S(2)}, u32[]{:S(2)}) collective-permute-start(bf16[72,4608]{1,0:T(8,128)(2,1)} %collective-permute-done.12), channel_id=1, source_target_pairs={{0,15},{1,0},{2,1},{3,2},{4,3},{5,4},{6,5},{7,6},{8,7},{9,8},{10,9... | collective-permute-start | bytes 1990664 | tf_op jit(solution)/shard_map/ppermute | solution.py:19
  234.3 16.9 %collective-permute-start.7 = (bf16[72,4608]{1,0:T(8,128)(2,1)}, bf16[72,4608]{1,0:T(8,128)(2,1)S(1)}, u32[]{:S(2)}, u32[]{:S(2)}) collective-permute-start(bf16[72,4608]{1,0:T(8,128)(2,1)} %collective-permute-done.6), channel_id=1, source_target_pairs={{0,1},{1,2},{2,3},{3,4},{4,5},{5,6},{6,7},{7,8},{8,9},{9,10},{10,1... | collective-permute-start | bytes 1990664 | tf_op jit(solution)/shard_map/ppermute | solution.py:17
  246.4 27.3 %collective-permute-start.14 = (bf16[72,4608]{1,0:T(8,128)(2,1)S(1)}, bf16[72,4608]{1,0:T(8,128)(2,1)S(1)}, u32[]{:S(2)}, u32[]{:S(2)}) collective-permute-start(bf16[72,4608]{1,0:T(8,128)(2,1)S(1)} %collective-permute-done.13), channel_id=1, source_target_pairs={{0,15},{1,0},{2,1},{3,2},{4,3},{5,4},{6,5},{7,6},{8,7},{9,8},{10,9... | collective-permute-start | bytes 1990664 | tf_op jit(solution)/shard_map/ppermute | solution.py:19
  373.6 235.6 %reduce-scatter.17.cloned.1.call-start = ((), (), s32[]{:S(2)}) async-start(), calls=%async_computation.17 | async-start | bytes 6266880 | tf_op jit(solution)/shard_map/reduce_scatter | solution.py:285
  382.6 260.5 %reduce-scatter.11.cloned.1.call-start = ((), (), s32[]{:S(2)}) async-start(), calls=%async_computation.14 | async-start | bytes 5640192 | tf_op jit(solution)/shard_map/reduce_scatter | solution.py:285
  405.8 318.4 %reduce-scatter.13.cloned.1.call-start = ((), (), s32[]{:S(2)}) async-start(), calls=%async_computation.15 | async-start | bytes 5640192 | tf_op jit(solution)/shard_map/reduce_scatter | solution.py:285
  413.5 392.0 %reduce-scatter.7.cloned.1.call-start = ((), (), s32[]{:S(2)}) async-start(), calls=%async_computation.12 | async-start | bytes 5640192 | tf_op jit(solution)/shard_map/reduce_scatter | solution.py:285
  470.5 415.9 %reduce-scatter.9.cloned.1.call-start = ((), (), s32[]{:S(2)}) async-start(), calls=%async_computation.13 | async-start | bytes 5640192 | tf_op jit(solution)/shard_map/reduce_scatter | solution.py:285
  484.0 491.8 %all-reduce.16.cloned.1.call-start = ((), (), s32[]{:S(2)}) async-start(), calls=%async_computation.18 | async-start | bytes 147456
  609.1 453.7 %all-reduce.18.cloned.1.call-start = ((), (), s32[]{:S(2)}) async-start(), calls=%async_computation.19 | async-start | bytes 5971968 | tf_op jit(solution)/shard_map/psum | solution.py:298
  611.3 281.5 %copy-start.5 = (bf16[2,256,1152]{2,1,0:T(8,128)(2,1)S(1)}, bf16[2,256,1152]{2,1,0:T(8,128)(2,1)}, u32[]{:S(2)}) copy-start(bf16[2,256,1152]{2,1,0:T(8,128)(2,1)} %param.14) | copy-start | bytes 3538948
  (67 other events, 1220.9 us)
Sparse Core Ops, SparseCore 0:
  10.2 108.7 all-gather.5
  121.2 41.8 all-gather.7
  165.4 115.8 all-gather.9
  283.4 95.3 all-gather.11
  382.6 92.6 reduce-scatter.14
  479.1 82.2 reduce-scatter.16
  565.5 77.5 reduce-scatter.10
  647.1 77.1 reduce-scatter.12
  728.3 77.0 reduce-scatter.6
  809.3 77.0 reduce-scatter.8
  889.9 85.8 all-reduce.15
  979.4 83.3 all-reduce.17
